TPU v7x, 32 devices: a whole 2x2x4 slice. The times are simulated.
32 devices in a mesh: tile: 16 (over z, y, x), mode: 2 (over core).
Axes of the slice: x: 2, y: 2, z: 4, core: 2. Of those that a mesh axis runs over, the one named last changes fastest.
Arguments:
- obj: float32 [16, 2, 384, 384], P('tile'), may hold values from -6 to 6
- probe: float32 [4, 2, 256, 256], P('mode'), may hold values from -3 to 3
- mode_weights: float32 [8, 4], P(None, 'mode'), may hold values from 0.25 to 1
- measured: float32 [64, 256, 256], P('tile'), may hold values from 0 to 4
- corner: int32 [64, 2], P('tile'), may hold values from 0 to 383, as said below
- counts: int32 [16], P('tile'), may hold values from 1 to 4, 32 in all
- weight_index: int32 [64], P('tile'), may hold values from 0 to 7
Outputs:
- obj_new: float32 [16, 2, 384, 384], P('tile')
- probe_new: float32 [4, 2, 256, 256], P('mode')
Inputs may be any that keep to these rules, and one draw needn't show every extreme that they name: Tile t has live slots 0 to counts[t] - 1 of its block; the counts sum to 32 and some tile has 4. The first slot of every tile has both corner coordinates between 192 and 320.
All inputs are finite; a program needn't handle non-finite values.
Results may differ from a plain program's by a relative error of at most 0.019.
The roundings to bfloat16 on the way count: a program that leaves them out, or rounds other values in their place, can miss the bound.
Values may be sent and summed in bfloat16 or wider, within the bound.
No kernel may reach another device: no remote copies, remote signals or barrier semaphores. Data moves between devices by JAX's collectives and lax.ppermute only.
A program may use at most 64 MiB of HBM per device.

v0:
```python
import math
import jax
import jax.numpy as jnp
from jax import lax
from jax.sharding import PartitionSpec as P

GC = 8
POS_DEV = 2
ITERS = 2
step_object = 0.1
step_probe = 4.0


def shifted(array, axis, by):
    peers = lax.axis_size(axis)
    return lax.ppermute(array, axis, [(i, (i + by) % peers) for i in range(peers)])


def dft_tables(length, sign):
    index = jnp.arange(length, dtype=jnp.int32)
    product = index[:, None] * index[None, :] % length
    angle = product.astype(jnp.float32) * (2.0 * math.pi / length)
    factor = 1.0 / math.sqrt(length)
    real = jnp.cos(angle) * factor
    imag = sign * jnp.sin(angle) * factor
    left = jnp.concatenate(
        [jnp.concatenate([real, -imag], 1), jnp.concatenate([imag, real], 1)], 0
    ).astype(jnp.bfloat16)
    right = jnp.concatenate([real, imag], 1).astype(jnp.bfloat16)
    return (left, right)


def transform(field, tables):
    left, right = tables
    count = field.shape[0]
    length = field.shape[-1]
    first = jnp.einsum(
        "ij,bjk->bik",
        left,
        field.reshape(count, 2 * length, length),
        preferred_element_type=jnp.float32,
    )
    first = first.astype(jnp.bfloat16).reshape(count, 2, length, length)
    second = jnp.einsum("bcjk,kl->bcjl", first, right, preferred_element_type=jnp.float32)
    real = second[:, 0, :, :length] - second[:, 1, :, length:]
    imag = second[:, 0, :, length:] + second[:, 1, :, :length]
    return jnp.stack([real, imag], 1)


def patch_contributions(
    object_patches, measured, active_mask, mode_weighting, probe, forward_pass, backward_pass, total
):
    count = object_patches.shape[0]
    modes = probe.shape[0]
    length = probe.shape[-1]
    obj_part = object_patches.astype(jnp.float32)[:, None]
    probe_part = probe[None]
    exit_real = probe_part[:, :, 0] * obj_part[:, :, 0] - probe_part[:, :, 1] * obj_part[:, :, 1]
    exit_imag = probe_part[:, :, 0] * obj_part[:, :, 1] + probe_part[:, :, 1] * obj_part[:, :, 0]
    exit_wave = jnp.stack([exit_real, exit_imag], 2).astype(jnp.bfloat16)
    psi = transform(exit_wave.reshape(count * modes, 2, length, length), forward_pass).reshape(
        count, modes, 2, length, length
    )
    power = psi[:, :, 0] * psi[:, :, 0] + psi[:, :, 1] * psi[:, :, 1]
    intensity = total(jnp.sum(mode_weighting[:, :, None, None] * power, 1))
    resid = (intensity - measured) * active_mask[:, None, None]
    scaled = (mode_weighting[:, :, None, None, None] * resid[:, None, None] * psi).astype(
        jnp.bfloat16
    )
    chi = transform(scaled.reshape(count * modes, 2, length, length), backward_pass).reshape(
        count, modes, 2, length, length
    )
    obj_real = jnp.sum(probe_part[:, :, 0] * chi[:, :, 0] + probe_part[:, :, 1] * chi[:, :, 1], 1)
    obj_imag = jnp.sum(probe_part[:, :, 0] * chi[:, :, 1] - probe_part[:, :, 1] * chi[:, :, 0], 1)
    probe_real = jnp.sum(obj_part[:, :, 0] * chi[:, :, 0] + obj_part[:, :, 1] * chi[:, :, 1], 0)
    probe_imag = jnp.sum(obj_part[:, :, 0] * chi[:, :, 1] - obj_part[:, :, 1] * chi[:, :, 0], 0)
    return (jnp.stack([obj_real, obj_imag], 1), jnp.stack([probe_real, probe_imag], 1))


def unchanged(value):
    return value


def body(obj, probe, mode_weights, measured, corner, counts, weight_index):
    patch = probe.shape[-1]
    tile = obj.shape[-1]
    capacity = measured.shape[0]
    kinds = mode_weights.shape[0]
    zero_index = jnp.zeros((), jnp.int32)
    forward_pass = dft_tables(patch, -1.0)
    backward_pass = dft_tables(patch, 1.0)
    active_mask = (jnp.arange(capacity, dtype=jnp.int32) < counts[0]).astype(jnp.float32)
    onehot = (weight_index[:, None] == jnp.arange(kinds, dtype=jnp.int32)[None, :]).astype(
        jnp.float32
    )
    positions = POS_DEV * lax.axis_size("tile")
    state = obj[0]
    probe_now = probe
    for sweep in range(ITERS):
        half = state.astype(jnp.bfloat16)
        right = shifted(half[:, :, :patch], "tile", -1)
        wide = jnp.concatenate([half, right], 2)
        below = shifted(half[:, :patch, :], "tile", -GC)
        diagonal = shifted(half[:, :patch, :patch], "tile", -(GC + 1))
        lower = jnp.concatenate([below, diagonal], 2)
        padded = jnp.concatenate([wide, lower], 1)

        def cut(spot):
            return lax.dynamic_slice(padded, (zero_index, spot[0], spot[1]), (2, patch, patch))

        object_patches = jax.vmap(cut)(corner)
        groups = lax.axis_size("mode")
        mine = lax.axis_index("mode")

        def pick(array):
            shaped = array.reshape((capacity // groups, groups) + array.shape[1:])
            return lax.dynamic_index_in_dim(shaped, mine, 1, keepdims=False)

        all_probe, all_weights = (
            lax.all_gather(probe_now, "mode", axis=0, tiled=True),
            lax.all_gather(mode_weights, "mode", axis=1, tiled=True),
        )
        mode_weighting = jnp.dot(pick(onehot), all_weights, precision=lax.Precision.HIGHEST)
        object_terms, probe_updates = patch_contributions(
            pick(object_patches),
            pick(measured),
            pick(active_mask),
            mode_weighting,
            all_probe,
            forward_pass,
            backward_pass,
            unchanged,
        )
        probe_updates = lax.psum_scatter(
            probe_updates.astype(jnp.bfloat16), "mode", scatter_dimension=0, tiled=True
        ).astype(jnp.float32)
        slot_corner = pick(corner)

        def place(slot, acc):
            spot = slot_corner[slot]
            where = (zero_index, spot[0], spot[1])
            current = lax.dynamic_slice(acc, where, (2, patch, patch))
            return lax.dynamic_update_slice(acc, current + object_terms[slot], where)

        gradient = jnp.zeros((2, tile + patch, tile + patch), jnp.float32)
        gradient = lax.fori_loop(0, object_terms.shape[0], place, gradient)
        above = shifted(gradient[:, tile:, :tile].astype(jnp.bfloat16), "tile", GC).astype(
            jnp.float32
        )
        upper_left = shifted(gradient[:, tile:, tile:].astype(jnp.bfloat16), "tile", GC + 1).astype(
            jnp.float32
        )
        gradient = gradient.at[:, :patch, :tile].add(above)
        gradient = gradient.at[:, :patch, :patch].add(upper_left)
        from_left = shifted(gradient[:, :tile, tile:].astype(jnp.bfloat16), "tile", 1).astype(
            jnp.float32
        )
        tile_grad = gradient[:, :tile, :tile].at[:, :, :patch].add(from_left)
        tile_grad = lax.psum(tile_grad.astype(jnp.bfloat16), "mode").astype(jnp.float32)
        probe_grad = lax.psum(probe_updates, "tile")
        state = state - step_object * tile_grad
        probe_now = probe_now - step_probe / positions * probe_grad
    return (state[None], probe_now)


def solution(mesh):
    placed = (
        P("tile", None, None, None),
        P("mode", None, None, None),
        P(None, "mode"),
        P("tile", None, None),
        P("tile", None),
        P("tile"),
        P("tile"),
    )
    return jax.shard_map(
        body,
        mesh=mesh,
        in_specs=placed,
        out_specs=(P("tile", None, None, None), P("mode", None, None, None)),
        check_vma=False,
    )
```

profile of v0, /device:TPU:0, one launch (start us, length us, event | category | flops | bytes accessed | tf_op | source)
XLA Modules:
  0.0 576.5 jit_solution(13252138141887793834)
XLA Ops:
  8.6 7.0 %collective-permute-start = (bf16[2,384,256]{2,1,0:T(8,128)(2,1)S(1)}, bf16[2,384,256]{2,1,0:T(8,128)(2,1)S(1)}, u32[]{:S(2)}, u32[]{:S(2)}) collective-permute-start(bf16[2,384,256]{2,1,0:T(8,128)(2,1)S(1)} %slice.449), channel_id=1, source_target_pairs={{0,30},{2,0},{4,2},{6,4},{8,6},{10,8},{12,10},{14,12},{16,14},{18,... | collective-permute-start | bytes 1179656 | tf_op jit(solution)/shard_map/ppermute | solution.py:16
  25.1 17.7 %collective-permute-done.2 = bf16[2,256,256]{2,1,0:T(8,128)(2,1)S(1)} collective-permute-done((bf16[2,256,256]{2,1,0:T(8,128)(2,1)S(1)}, bf16[2,256,256]{2,1,0:T(8,128)(2,1)S(1)}, u32[]{:S(2)}, u32[]{:S(2)}) %collective-permute-start.2) | collective-permute-done | bytes 262176 | tf_op jit(solution)/shard_map/ppermute | solution.py:16
  42.8 3.6 collective-permute-done.1
  46.6 8.3 %while.36 = (s32[]{:T(128)}, bf16[2,640,640]{2,1,0:T(8,128)(2,1)S(1)}, s32[4,3]{1,0:T(4,128)S(1)}, bf16[4,2,256,256]{3,2,1,0:T(8,128)(2,1)S(1)}, s32[]{:T(128)}) while((s32[]{:T(128)}, bf16[2,640,640]{2,1,0:T(8,128)(2,1)S(1)}, s32[4,3]{1,0:T(4,128)S(1)}, bf16[4,2,256,256]{3,2,1,0:T(8,128)(2,1)S(1)}, s32[]{:T(128)}) %tuple.139), condition=%wide.while_cond.6, body=%wide.while_body.6.sunk | while | flops 2 | bytes 524405 | solution.py:109
  60.8 5.5 subtract_convert_fusion.1
  66.3 4.8 pad_maximum_fusion
  71.1 2.7 convert_element_type.143
  73.8 4.2 convert_bitcast_fusion.3
  78.0 2.8 copy.47
  86.5 4.9 copy.36
  91.4 2.7 convert_element_type.149
  94.1 4.2 convert_bitcast_fusion.2
  98.3 3.4 copy.48
  107.6 24.8 %while.34 = (s32[]{:T(128)}, f32[2,640,640]{2,1,0:T(8,128)}, s32[2,2]{1,0:T(2,128)S(1)}, f32[2,2,256,256]{3,2,1,0:T(8,128)S(1)}, s32[]{:T(128)}, /*index=5*/s32[]{:T(128)}, s32[]{:T(128)}) while((s32[]{:T(128)}, f32[2,640,640]{2,1,0:T(8,128)}, s32[2,2]{1,0:T(2,128)S(1)}, f32[2,2,256,256]{3,2,1,0:T(8,128)S(1)}, s32[]{:T(128)}, ...), condition=%wide.region_4.5_spmd, body=%wide.region_3.4_spmd.sunk | while | flops 131080 | bytes 2621637 | solution.py:146
  113.5 6.3 %dynamic_update_slice.16 = f32[2,640,640]{2,1,0:T(8,128)} dynamic-update-slice(f32[2,640,640]{2,1,0:T(8,128)} %get-tuple-element.475, f32[2,256,256]{2,1,0:T(8,128)S(1)} %bitcast_add_fusion.4, s32[]{:T(128)} %constant.258.clone.1..sunk, s32[]{:T(128)S(6)} %select_n.129, s32[]{:T(128)S(6)} %select_n.130) | dynamic-update-slice | bytes 1048580 | tf_op jit(solution)/shard_map/while/body/eval_jaxpr/dynamic_update_slice | solution.py:143
  125.7 6.8 %dynamic_update_slice.16 = f32[2,640,640]{2,1,0:T(8,128)} dynamic-update-slice(f32[2,640,640]{2,1,0:T(8,128)} %get-tuple-element.475, f32[2,256,256]{2,1,0:T(8,128)S(1)} %bitcast_add_fusion.4, s32[]{:T(128)} %constant.258.clone.1..sunk, s32[]{:T(128)S(6)} %select_n.129, s32[]{:T(128)S(6)} %select_n.130) | dynamic-update-slice | bytes 1048580 | tf_op jit(solution)/shard_map/while/body/eval_jaxpr/dynamic_update_slice | solution.py:143
  132.5 2.2 convert.89
  136.1 24.7 %collective-permute-done.3 = bf16[2,256,384]{2,1,0:T(8,128)(2,1)S(1)} collective-permute-done((bf16[2,256,384]{2,1,0:T(8,128)(2,1)S(1)}, bf16[2,256,384]{2,1,0:T(8,128)(2,1)S(1)}, u32[]{:S(2)}, u32[]{:S(2)}) %collective-permute-start.3) | collective-permute-done | bytes 393248 | tf_op jit(solution)/shard_map/ppermute | solution.py:16
  161.2 5.9 %collective-permute-start.5 = (bf16[2,384,256]{2,1,0:T(8,128)(2,1)S(1)}, bf16[2,384,256]{2,1,0:T(8,128)(2,1)S(1)}, u32[]{:S(2)}, u32[]{:S(2)}) collective-permute-start(bf16[2,384,256]{2,1,0:T(8,128)(2,1)S(1)} %slice.531), channel_id=1, source_target_pairs={{0,2},{2,4},{4,6},{6,8},{8,10},{10,12},{12,14},{14,16},{16,18},{18... | collective-permute-start | bytes 1179656 | tf_op jit(solution)/shard_map/ppermute | solution.py:16
  167.2 7.6 %collective-permute-done.5 = bf16[2,384,256]{2,1,0:T(8,128)(2,1)S(1)} collective-permute-done((bf16[2,384,256]{2,1,0:T(8,128)(2,1)S(1)}, bf16[2,384,256]{2,1,0:T(8,128)(2,1)S(1)}, u32[]{:S(2)}, u32[]{:S(2)}) %collective-permute-start.5) | collective-permute-done | bytes 393248 | tf_op jit(solution)/shard_map/ppermute | solution.py:16
  176.9 17.3 %all-reduce.5.cloned.1.call-done = bf16[2,384,384]{2,1,0:T(8,128)(2,1)} async-done(((bf16[2,384,384]{2,1,0:T(8,128)(2,1)}), bf16[2,384,384]{2,1,0:T(8,128)(2,1)}) %all-reduce.5.cloned.1.call-update) | async-done | bytes 589840 | tf_op jit(solution)/shard_map/psum | solution.py:159
  197.8 5.4 collective-permute-start.6
  204.4 2.3 reduce-scatter.3.cloned.1.call-done
  206.7 103.1 %all-reduce.8 = f32[2,2,256,256]{3,2,1,0:T(8,128)} all-reduce(bf16[2,2,256,256]{3,2,1,0:T(8,128)(2,1)} %reduce-scatter.3.cloned.1.call-done), channel_id=1, replica_groups=mesh['tile'=16,'mode'=2] {'tile'}, use_global_device_ids=true, to_apply=%region_9.10 | all-reduce | flops 262144 | bytes 1572864 | tf_op jit(solution)/shard_map/psum | solution.py:160
  309.8 2.4 multiply_subtract_fusion.1
  315.4 11.3 %while.37 = (s32[]{:T(128)}, bf16[2,640,640]{2,1,0:T(8,128)(2,1)S(1)}, s32[4,3]{1,0:T(4,128)S(1)}, bf16[4,2,256,256]{3,2,1,0:T(8,128)(2,1)}, s32[]{:T(128)}) while((s32[]{:T(128)}, bf16[2,640,640]{2,1,0:T(8,128)(2,1)S(1)}, s32[4,3]{1,0:T(4,128)S(1)}, bf16[4,2,256,256]{3,2,1,0:T(8,128)(2,1)}, s32[]{:T(128)}) %tuple.163), condition=%wide.while_cond.7, body=%wide.while_body.7.sunk | while | flops 2 | bytes 525929 | solution.py:109
  316.2 2.2 bitcast_dynamic-update-slice_fusion.5
  334.9 5.7 subtract_convert_fusion
  340.6 4.8 pad_maximum_fusion.1
  345.5 2.7 convert_element_type.160
  348.1 4.2 convert_bitcast_fusion.1
  352.3 2.8 copy.49
  360.8 4.9 copy.43
  365.7 2.7 convert_element_type.164
  368.4 4.2 convert_bitcast_fusion
  372.6 3.1 copy.50
  378.7 2.2 fusion.7
  382.9 24.8 %while.35 = (s32[]{:T(128)}, f32[2,640,640]{2,1,0:T(8,128)}, s32[2,2]{1,0:T(2,128)S(1)}, f32[2,2,256,256]{3,2,1,0:T(8,128)S(1)}, s32[]{:T(128)}, /*index=5*/s32[]{:T(128)}, s32[]{:T(128)}) while((s32[]{:T(128)}, f32[2,640,640]{2,1,0:T(8,128)}, s32[2,2]{1,0:T(2,128)S(1)}, f32[2,2,256,256]{3,2,1,0:T(8,128)S(1)}, s32[]{:T(128)}, ...), condition=%wide.region_14.15_spmd, body=%wide.region_13.14_spmd.sunk | while | flops 131080 | bytes 2621637 | solution.py:146
  388.7 6.3 %dynamic_update_slice.17 = f32[2,640,640]{2,1,0:T(8,128)} dynamic-update-slice(f32[2,640,640]{2,1,0:T(8,128)} %get-tuple-element.511, f32[2,256,256]{2,1,0:T(8,128)S(1)} %bitcast_add_fusion.5, s32[]{:T(128)} %constant.258.clone.1..sunk.1, s32[]{:T(128)S(6)} %select_n.131, s32[]{:T(128)S(6)} %select_n.132) | dynamic-update-slice | bytes 1048580 | tf_op jit(solution)/shard_map/while/body/eval_jaxpr/dynamic_update_slice | solution.py:143
  400.9 6.8 %dynamic_update_slice.17 = f32[2,640,640]{2,1,0:T(8,128)} dynamic-update-slice(f32[2,640,640]{2,1,0:T(8,128)} %get-tuple-element.511, f32[2,256,256]{2,1,0:T(8,128)S(1)} %bitcast_add_fusion.5, s32[]{:T(128)} %constant.258.clone.1..sunk.1, s32[]{:T(128)S(6)} %select_n.131, s32[]{:T(128)S(6)} %select_n.132) | dynamic-update-slice | bytes 1048580 | tf_op jit(solution)/shard_map/while/body/eval_jaxpr/dynamic_update_slice | solution.py:143
  407.7 2.2 convert.95
  410.7 17.1 %collective-permute-done.9 = bf16[2,256,384]{2,1,0:T(8,128)(2,1)S(1)} collective-permute-done((bf16[2,256,384]{2,1,0:T(8,128)(2,1)S(1)}, bf16[2,256,384]{2,1,0:T(8,128)(2,1)S(1)}, u32[]{:S(2)}, u32[]{:S(2)}) %collective-permute-start.9) | collective-permute-done | bytes 393248 | tf_op jit(solution)/shard_map/ppermute | solution.py:16
  428.2 5.5 collective-permute-start.11
  433.8 13.2 %collective-permute-done.11 = bf16[2,384,256]{2,1,0:T(8,128)(2,1)S(1)} collective-permute-done((bf16[2,384,256]{2,1,0:T(8,128)(2,1)S(1)}, bf16[2,384,256]{2,1,0:T(8,128)(2,1)S(1)}, u32[]{:S(2)}, u32[]{:S(2)}) %collective-permute-start.11) | collective-permute-done | bytes 393248 | tf_op jit(solution)/shard_map/ppermute | solution.py:16
  449.1 15.8 %all-reduce.7.cloned.1.call-done = bf16[2,384,384]{2,1,0:T(8,128)(2,1)} async-done(((bf16[2,384,384]{2,1,0:T(8,128)(2,1)}), bf16[2,384,384]{2,1,0:T(8,128)(2,1)}) %all-reduce.7.cloned.1.call-update) | async-done | bytes 589840 | tf_op jit(solution)/shard_map/psum | solution.py:159
  464.9 2.3 subtract_bitcast_fusion
  467.2 10.0 %reduce-scatter.5.cloned.1.call-done = bf16[2,2,256,256]{3,2,1,0:T(8,128)(2,1)} async-done(((bf16[4,2,256,256]{3,2,1,0:T(8,128)(2,1)}), bf16[2,2,256,256]{3,2,1,0:T(8,128)(2,1)}) %reduce-scatter.5.cloned.1.call-update) | async-done | bytes 524304 | tf_op jit(solution)/shard_map/reduce_scatter | solution.py:134
  477.2 91.1 %all-reduce.9 = f32[2,2,256,256]{3,2,1,0:T(8,128)S(1)} all-reduce(bf16[2,2,256,256]{3,2,1,0:T(8,128)(2,1)} %reduce-scatter.5.cloned.1.call-done), channel_id=1, replica_groups=mesh['tile'=16,'mode'=2] {'tile'}, use_global_device_ids=true, to_apply=%region_19.20 | all-reduce | flops 262144 | bytes 1572864 | tf_op jit(solution)/shard_map/psum | solution.py:160
  (218 shorter events, 87.6 us)
Async XLA Ops:
  7.2 50.2 %all-gather.4.cloned.1.call-start = ((), (), s32[]{:S(2)}) async-start(), calls=%async_computation.2 | async-start | bytes 3145728 | tf_op jit(solution)/shard_map/all_gather | solution.py:120
  8.5 11.2 %copy-start.33 = (s32[4,2]{0,1:T(2,128)S(1)}, s32[4,2]{0,1:T(2,128)}, u32[]{:S(2)}) copy-start(s32[4,2]{0,1:T(2,128)} %param.27) | copy-start | bytes 100
  8.6 11.4 %copy-start.35 = (s32[4]{0:T(128)S(1)}, s32[4]{0:T(128)}, u32[]{:S(2)}) copy-start(s32[4]{0:T(128)} %param.29) | copy-start | bytes 52
  8.6 11.6 %copy-start.34 = (f32[8,2]{0,1:T(2,128)S(1)}, f32[8,2]{0,1:T(2,128)}, u32[]{:S(2)}) copy-start(f32[8,2]{0,1:T(2,128)} %param.25) | copy-start | bytes 196
  8.6 34.2 %collective-permute-start = (bf16[2,384,256]{2,1,0:T(8,128)(2,1)S(1)}, bf16[2,384,256]{2,1,0:T(8,128)(2,1)S(1)}, u32[]{:S(2)}, u32[]{:S(2)}) collective-permute-start(bf16[2,384,256]{2,1,0:T(8,128)(2,1)S(1)} %slice.449), channel_id=1, source_target_pairs={{0,30},{2,0},{4,2},{6,4},{8,6},{10,8},{12,10},{14,12},{16,14},{18,... | collective-permute-start | bytes 1179656 | tf_op jit(solution)/shard_map/ppermute | solution.py:16
  15.7 30.7 %collective-permute-start.1 = (bf16[2,256,384]{2,1,0:T(8,128)(2,1)S(1)}, bf16[2,256,384]{2,1,0:T(8,128)(2,1)S(1)}, u32[]{:S(2)}, u32[]{:S(2)}) collective-permute-start(bf16[2,256,384]{2,1,0:T(8,128)(2,1)S(1)} %slice.450), channel_id=1, source_target_pairs={{0,16},{2,18},{4,20},{6,22},{8,24},{10,26},{12,28},{14,30},{16,0},... | collective-permute-start | bytes 1179656 | tf_op jit(solution)/shard_map/ppermute | solution.py:16
  15.8 27.0 %collective-permute-start.2 = (bf16[2,256,256]{2,1,0:T(8,128)(2,1)S(1)}, bf16[2,256,256]{2,1,0:T(8,128)(2,1)S(1)}, u32[]{:S(2)}, u32[]{:S(2)}) collective-permute-start(bf16[2,256,256]{2,1,0:T(8,128)(2,1)S(1)} %slice.451), channel_id=1, source_target_pairs={{0,14},{2,16},{4,18},{6,20},{8,22},{10,24},{12,26},{14,28},{16,30}... | collective-permute-start | bytes 786440 | tf_op jit(solution)/shard_map/ppermute | solution.py:16
  16.9 177.3 %all-reduce.5.cloned.1.call-start = ((), (), s32[]{:S(2)}) async-start(), calls=%async_computation.3 | async-start | bytes 1179648 | tf_op jit(solution)/shard_map/psum | solution.py:159
  19.7 61.1 %copy-start.24 = (bf16[256,256]{1,0:T(8,128)(2,1)}, bf16[256,256]{1,0:T(8,128)(2,1)S(1)}, u32[]{:S(2)}) copy-start(bf16[256,256]{1,0:T(8,128)(2,1)S(1)} %multiply_convert_fusion.2) | copy-start | bytes 393220
  55.1 2.2 copy-start.14
  55.1 2.2 copy-start.16
  59.1 1.7 copy-start.8
  71.1 2.7 copy-start.31
  83.0 1.2 copy-start.28
  91.4 2.7 copy-start.26
  91.4 2.7 copy-start.32
  102.9 1.3 copy-start.15
  102.9 1.5 copy-start.17
  132.5 28.4 %copy-start.1 = (f32[2,640,640]{2,1,0:T(8,128)S(1)}, f32[2,640,640]{2,1,0:T(8,128)}, u32[]{:S(2)}) copy-start(f32[2,640,640]{2,1,0:T(8,128)} %get-tuple-element.232) | copy-start | bytes 9830404
  134.8 26.1 %collective-permute-start.3 = (bf16[2,256,384]{2,1,0:T(8,128)(2,1)S(1)}, bf16[2,256,384]{2,1,0:T(8,128)(2,1)S(1)}, u32[]{:S(2)}, u32[]{:S(2)}) collective-permute-start(bf16[2,256,384]{2,1,0:T(8,128)(2,1)S(1)} %slice.463), channel_id=1, source_target_pairs={{0,16},{2,18},{4,20},{6,22},{8,24},{10,26},{12,28},{14,30},{16,0},... | collective-permute-start | bytes 1179656 | tf_op jit(solution)/shard_map/ppermute | solution.py:16
  134.9 26.2 %collective-permute-start.4 = (bf16[2,256,256]{2,1,0:T(8,128)(2,1)S(1)}, bf16[2,256,256]{2,1,0:T(8,128)(2,1)S(1)}, u32[]{:S(2)}, u32[]{:S(2)}) collective-permute-start(bf16[2,256,256]{2,1,0:T(8,128)(2,1)S(1)} %slice.465), channel_id=1, source_target_pairs={{0,18},{2,20},{4,22},{6,24},{8,26},{10,28},{12,30},{14,0},{16,2},{... | collective-permute-start | bytes 786440 | tf_op jit(solution)/shard_map/ppermute | solution.py:16
  161.2 13.6 %collective-permute-start.5 = (bf16[2,384,256]{2,1,0:T(8,128)(2,1)S(1)}, bf16[2,384,256]{2,1,0:T(8,128)(2,1)S(1)}, u32[]{:S(2)}, u32[]{:S(2)}) collective-permute-start(bf16[2,384,256]{2,1,0:T(8,128)(2,1)S(1)} %slice.531), channel_id=1, source_target_pairs={{0,2},{2,4},{4,6},{6,8},{8,10},{10,12},{12,14},{14,16},{16,18},{18... | collective-permute-start | bytes 1179656 | tf_op jit(solution)/shard_map/ppermute | solution.py:16
  174.9 19.3 %copy-start.2 = (f32[1,2,384,384]{3,2,1,0:T(8,128)S(1)}, f32[1,2,384,384]{3,2,1,0:T(8,128)}, u32[]{:S(2)}) copy-start(f32[1,2,384,384]{3,2,1,0:T(8,128)} %param.23) | copy-start | bytes 3538948
  175.8 31.0 %reduce-scatter.3.cloned.1.call-start = ((), (), s32[]{:S(2)}) async-start(), calls=%async_computation.4 | async-start | bytes 1572864 | tf_op jit(solution)/shard_map/reduce_scatter | solution.py:134
  176.9 153.3 %all-gather.6.cloned.1.call-start = ((), (), s32[]{:S(2)}) async-start(), calls=%async_computation.5 | async-start | bytes 3145728 | tf_op jit(solution)/shard_map/all_gather | solution.py:120
  195.5 114.3 %copy-start.18 = (f32[2,2,256,256]{3,2,1,0:T(8,128)S(1)}, f32[2,2,256,256]{3,2,1,0:T(8,128)}, u32[]{:S(2)}) copy-start(f32[2,2,256,256]{3,2,1,0:T(8,128)} %param.24) | copy-start | bytes 3145732
  197.8 114.5 %collective-permute-start.6 = (bf16[2,384,256]{2,1,0:T(8,128)(2,1)}, bf16[2,384,256]{2,1,0:T(8,128)(2,1)S(1)}, u32[]{:S(2)}, u32[]{:S(2)}) collective-permute-start(bf16[2,384,256]{2,1,0:T(8,128)(2,1)} %slice.470), channel_id=1, source_target_pairs={{0,30},{2,0},{4,2},{6,4},{8,6},{10,8},{12,10},{14,12},{16,14},{18,... | collective-permute-start | bytes 1179656 | tf_op jit(solution)/shard_map/ppermute | solution.py:16
  203.3 109.8 %collective-permute-start.7 = (bf16[2,256,384]{2,1,0:T(8,128)(2,1)}, bf16[2,256,384]{2,1,0:T(8,128)(2,1)}, u32[]{:S(2)}, u32[]{:S(2)}) collective-permute-start(bf16[2,256,384]{2,1,0:T(8,128)(2,1)} %slice.471), channel_id=1, source_target_pairs={{0,16},{2,18},{4,20},{6,22},{8,24},{10,26},{12,28},{14,30},{16,0},... | collective-permute-start | bytes 1179656 | tf_op jit(solution)/shard_map/ppermute | solution.py:16
  203.3 109.0 %collective-permute-start.8 = (bf16[2,256,256]{2,1,0:T(8,128)(2,1)}, bf16[2,256,256]{2,1,0:T(8,128)(2,1)}, u32[]{:S(2)}, u32[]{:S(2)}) collective-permute-start(bf16[2,256,256]{2,1,0:T(8,128)(2,1)} %slice.472), channel_id=1, source_target_pairs={{0,14},{2,16},{4,18},{6,20},{8,22},{10,24},{12,26},{14,28},{16,30}... | collective-permute-start | bytes 786440 | tf_op jit(solution)/shard_map/ppermute | solution.py:16
  312.2 152.7 %all-reduce.7.cloned.1.call-start = ((), (), s32[]{:S(2)}) async-start(), calls=%async_computation.6 | async-start | bytes 1179648 | tf_op jit(solution)/shard_map/psum | solution.py:159
  328.0 2.2 copy-start.10
  328.0 2.2 copy-start.12
  332.0 3.0 copy-start.4
  332.0 3.0 copy-start.6
  345.4 2.7 copy-start.25
  365.7 2.7 copy-start.27
  376.9 1.5 copy-start.7
  376.9 1.7 copy-start.11
  376.9 1.8 copy-start.13
  407.7 20.1 %copy-start = (f32[2,640,640]{2,1,0:T(8,128)S(1)}, f32[2,640,640]{2,1,0:T(8,128)}, u32[]{:S(2)}) copy-start(f32[2,640,640]{2,1,0:T(8,128)} %get-tuple-element.233) | copy-start | bytes 9830404
  410.0 17.8 %collective-permute-start.9 = (bf16[2,256,384]{2,1,0:T(8,128)(2,1)S(1)}, bf16[2,256,384]{2,1,0:T(8,128)(2,1)S(1)}, u32[]{:S(2)}, u32[]{:S(2)}) collective-permute-start(bf16[2,256,384]{2,1,0:T(8,128)(2,1)S(1)} %slice.484), channel_id=1, source_target_pairs={{0,16},{2,18},{4,20},{6,22},{8,24},{10,26},{12,28},{14,30},{16,0},... | collective-permute-start | bytes 1179656 | tf_op jit(solution)/shard_map/ppermute | solution.py:16
  410.1 18.0 %collective-permute-start.10 = (bf16[2,256,256]{2,1,0:T(8,128)(2,1)S(1)}, bf16[2,256,256]{2,1,0:T(8,128)(2,1)S(1)}, u32[]{:S(2)}, u32[]{:S(2)}) collective-permute-start(bf16[2,256,256]{2,1,0:T(8,128)(2,1)S(1)} %slice.486), channel_id=1, source_target_pairs={{0,18},{2,20},{4,22},{6,24},{8,26},{10,28},{12,30},{14,0},{16,2},{... | collective-permute-start | bytes 786440 | tf_op jit(solution)/shard_map/ppermute | solution.py:16
  428.1 19.9 %copy-start.22 = (bf16[4,256,256]{2,1,0:T(8,128)(2,1)S(1)}, bf16[4,256,256]{2,1,0:T(8,128)(2,1)}, u32[]{:S(2)}) copy-start(bf16[4,256,256]{2,1,0:T(8,128)(2,1)} %get-tuple-element.254) | copy-start | bytes 1572868
  428.2 19.9 %copy-start.23 = (bf16[4,256,256]{2,1,0:T(8,128)(2,1)S(1)}, bf16[4,256,256]{2,1,0:T(8,128)(2,1)}, u32[]{:S(2)}) copy-start(bf16[4,256,256]{2,1,0:T(8,128)(2,1)} %get-tuple-element.255) | copy-start | bytes 1572868
  428.2 18.8 %collective-permute-start.11 = (bf16[2,384,256]{2,1,0:T(8,128)(2,1)S(1)}, bf16[2,384,256]{2,1,0:T(8,128)(2,1)S(1)}, u32[]{:S(2)}, u32[]{:S(2)}) collective-permute-start(bf16[2,384,256]{2,1,0:T(8,128)(2,1)S(1)} %slice.530), channel_id=1, source_target_pairs={{0,2},{2,4},{4,6},{6,8},{8,10},{10,12},{12,14},{14,16},{16,18},{18... | collective-permute-start | bytes 1179656 | tf_op jit(solution)/shard_map/ppermute | solution.py:16
  447.1 17.8 %copy-start.19 = (bf16[2,384,384]{2,1,0:T(8,128)(2,1)S(1)}, bf16[2,384,384]{2,1,0:T(8,128)(2,1)}, u32[]{:S(2)}) copy-start(bf16[2,384,384]{2,1,0:T(8,128)(2,1)} %all-reduce.5.cloned.1.call-done) | copy-start | bytes 1769476
  448.0 29.3 %reduce-scatter.5.cloned.1.call-start = ((), (), s32[]{:S(2)}) async-start(), calls=%async_computation.7 | async-start | bytes 1572864 | tf_op jit(solution)/shard_map/reduce_scatter | solution.py:134
  449.1 119.2 %copy-start.3 = (f32[2,2,256,256]{3,2,1,0:T(8,128)S(1)}, f32[2,2,256,256]{3,2,1,0:T(8,128)}, u32[]{:S(2)}) copy-start(f32[2,2,256,256]{3,2,1,0:T(8,128)} %multiply_subtract_fusion.1) | copy-start | bytes 3145732
  (6 other events, 6.1 us)
Sparse Core Ops, SparseCore 0:
  17.1 9.6 all-gather.3
  175.9 18.3 all-reduce.4
  197.1 9.5 reduce-scatter.2
  312.3 7.9 all-gather.5
  448.1 16.7 all-reduce.6
  467.6 9.5 reduce-scatter.4
where the time goes:
time: 582 us; the launch traced here: 576 us
  blocking collectives  196 us (34%)
  waiting for transfers between devices  129 us (22%)
  local copies, waits for them, and re-layouts  108 us (19%)
  other arithmetic  61 us (10%)
  starting transfers between devices  28.5 us (5%)
  matrix products  22 us (4%)
  loops' own time  15.8 us (3%)
  between operations  15.8 us (3%)
    psum x2, blocking collectives, body(): probe_grad = lax.psum(probe_updates, 'tile')  194 us
    ppermute x12, waiting for transfers between devices, shifted(): lax.ppermute(array, axis, [(i, (i + by) % peers) for i in range(peers)])  83.9 us
    psum x2, waiting for transfers between devices, body(): lax.psum(tile_grad.astype(jnp.bfloat16), 'mode').astype(jnp.float32)  33.1 us
    ppermute x12, starting transfers between devices, shifted(): lax.ppermute(array, axis, [(i, (i + by) % peers) for i in range(peers)])  28.2 us
    dynamic_update_slice x4, local copies, waits for them, and re-layouts, place(): return lax.dynamic_update_slice(acc, current + object_terms[slot], where)  26.3 us
    another operation x7, other arithmetic  20.1 us
    gather x24, local copies, waits for them, and re-layouts  19.3 us
    dot_general x4, matrix products, transform(): jnp.einsum('ij,bjk->bik', left, field.reshape(count, 2 * length, length),...  16.8 us
  transfers between devices with their start and end apart: 18, of which 10 were waited for; matrix products, arithmetic and copies ran while one was open for 8% of the time, Pallas kernels for 0%

commit v1 on v0

--- a/solution.py
+++ b/solution.py
@@ -157,7 +157,8 @@
         )
         tile_grad = gradient[:, :tile, :tile].at[:, :, :patch].add(from_left)
         tile_grad = lax.psum(tile_grad.astype(jnp.bfloat16), "mode").astype(jnp.float32)
-        probe_grad = lax.psum(probe_updates, "tile")
+        parts = lax.all_gather(probe_updates, "tile", axis=0, tiled=False)
+        probe_grad = parts.sum(axis=0)
         state = state - step_object * tile_grad
         probe_now = probe_now - step_probe / positions * probe_grad
     return (state[None], probe_now)

time: 582 us -> 802 us (1.38)
  waiting for transfers between devices: 129 us -> 521 us
  blocking collectives: 196 us -> 2.09 us
  other arithmetic: 61 us -> 76 us
    all_gather x0 -> x2, waiting for transfers between devices: none -> 399 us  [body(): parts = lax.all_gather(probe_updates, 'tile', axis=0, tiled=False)]
    psum x2 -> x0, blocking collectives: 194 us -> none  [body(): probe_grad = lax.psum(probe_updates, 'tile')]
    reduce_sum x0 -> x2, other arithmetic: none -> 14.1 us  [body(): probe_grad = parts.sum(axis=0)]
    reduce_scatter x2 -> x0, waiting for transfers between devices: 12.3 us -> none  [body(): lax.psum_scatter(probe_updates.astype(jnp.bfloat16), 'mode', scatter_dime...]
  transfers between devices with their start and end apart: 18 -> 18, of which waited for: 10 -> 10; matrix products, arithmetic and copies ran while one was open for 8% -> 6% of each run, Pallas kernels for 0% -> 0%
where the time goes in v1:
time: 802 us; the launch traced here: 797 us
  waiting for transfers between devices  521 us (65%)
  local copies, waits for them, and re-layouts  110 us (14%)
  other arithmetic  76 us (9%)
  starting transfers between devices  32.6 us (4%)
  matrix products  22.1 us (3%)
  between operations  16.4 us (2%)
  loops' own time  15.8 us (2%)
    all_gather x2, waiting for transfers between devices, body(): parts = lax.all_gather(probe_updates, 'tile', axis=0, tiled=False)  399 us
    ppermute x12, waiting for transfers between devices, shifted(): lax.ppermute(array, axis, [(i, (i + by) % peers) for i in range(peers)])  85.1 us
    psum x2, waiting for transfers between devices, body(): lax.psum(tile_grad.astype(jnp.bfloat16), 'mode').astype(jnp.float32)  37.6 us
    ppermute x12, starting transfers between devices, shifted(): lax.ppermute(array, axis, [(i, (i + by) % peers) for i in range(peers)])  32.3 us
    dynamic_update_slice x4, local copies, waits for them, and re-layouts, place(): return lax.dynamic_update_slice(acc, current + object_terms[slot], where)  26.3 us
    gather x24, local copies, waits for them, and re-layouts  20.2 us
    another operation x7, other arithmetic  20.1 us
    dot_general x4, matrix products, transform(): jnp.einsum('ij,bjk->bik', left, field.reshape(count, 2 * length, length),...  16.9 us
  transfers between devices with their start and end apart: 18, of which 10 were waited for; matrix products, arithmetic and copies ran while one was open for 6% of the time, Pallas kernels for 0%

profile of v1, /device:TPU:0, one launch (start us, length us, event | category | flops | bytes accessed | tf_op | source)
XLA Modules:
  0.0 796.7 jit_solution(13131660799891368798)
XLA Ops:
  8.6 7.0 collective-permute-start
  25.1 17.7 %collective-permute-done.2 = bf16[2,256,256]{2,1,0:T(8,128)(2,1)S(1)} collective-permute-done((bf16[2,256,256]{2,1,0:T(8,128)(2,1)S(1)}, bf16[2,256,256]{2,1,0:T(8,128)(2,1)S(1)}, u32[]{:S(2)}, u32[]{:S(2)}) %collective-permute-start.2) | collective-permute-done | bytes 262176 | tf_op jit(solution)/shard_map/ppermute | solution.py:16
  42.8 3.6 collective-permute-done.1
  46.6 8.0 %while.36 = (s32[]{:T(128)}, bf16[2,640,640]{2,1,0:T(8,128)(2,1)S(1)}, s32[4,3]{1,0:T(4,128)S(1)}, bf16[4,2,256,256]{3,2,1,0:T(8,128)(2,1)S(1)}, s32[]{:T(128)}) while((s32[]{:T(128)}, bf16[2,640,640]{2,1,0:T(8,128)(2,1)S(1)}, s32[4,3]{1,0:T(4,128)S(1)}, bf16[4,2,256,256]{3,2,1,0:T(8,128)(2,1)S(1)}, s32[]{:T(128)}) %tuple.140), condition=%wide.while_cond.6, body=%wide.while_body.6.sunk | while | flops 2 | bytes 524405 | solution.py:109
  60.4 5.5 subtract_convert_fusion.1
  65.9 4.8 pad_maximum_fusion
  70.8 2.6 convert_element_type.139
  73.4 4.2 convert_bitcast_fusion.3
  77.6 2.8 copy.68
  86.0 4.9 copy.54
  90.9 2.6 convert_element_type.145
  93.5 4.2 convert_bitcast_fusion.2
  97.8 3.4 copy.69
  108.0 24.8 %while.34 = (s32[]{:T(128)}, f32[2,640,640]{2,1,0:T(8,128)}, s32[2,2]{1,0:T(2,128)S(1)}, f32[2,2,256,256]{3,2,1,0:T(8,128)S(1)}, s32[]{:T(128)}, /*index=5*/s32[]{:T(128)}, s32[]{:T(128)}) while((s32[]{:T(128)}, f32[2,640,640]{2,1,0:T(8,128)}, s32[2,2]{1,0:T(2,128)S(1)}, f32[2,2,256,256]{3,2,1,0:T(8,128)S(1)}, s32[]{:T(128)}, ...), condition=%wide.region_4.5_spmd, body=%wide.region_3.4_spmd.sunk | while | flops 131080 | bytes 2621637 | solution.py:146
  113.8 6.4 dynamic_update_slice.16
  126.0 6.8 dynamic_update_slice.16
  132.8 2.2 convert.91
  136.5 24.7 %collective-permute-done.3 = bf16[2,256,384]{2,1,0:T(8,128)(2,1)S(1)} collective-permute-done((bf16[2,256,384]{2,1,0:T(8,128)(2,1)S(1)}, bf16[2,256,384]{2,1,0:T(8,128)(2,1)S(1)}, u32[]{:S(2)}, u32[]{:S(2)}) %collective-permute-start.3) | collective-permute-done | bytes 393248 | tf_op jit(solution)/shard_map/ppermute | solution.py:16
  161.6 5.9 collective-permute-start.5
  168.6 6.6 collective-permute-done.5
  177.4 19.0 %all-reduce.9.cloned.1.call-done = (bf16[2,384,384]{2,1,0:T(8,128)(2,1)}, bf16[4,2,256,256]{3,2,0,1:T(8,128)(2,1)}) async-done(((bf16[2,384,384]{2,1,0:T(8,128)(2,1)}, bf16[4,2,256,256]{3,2,0,1:T(8,128)(2,1)}), (bf16[2,384,384]{2,1,0:T(8,128)(2,1)}, bf16[4,2,256,256]{3,2,0,1:T(8,128)(2,1)})) %all-reduce.9.cloned.1.call-update) | async-done | bytes 1638416 | tf_op jit(solution)/shard_map/psum | solution.py:159
  201.1 5.4 collective-permute-start.6
  207.7 206.6 %all-gather.12.cloned.1.call-done = f32[32,2,256,256]{3,2,0,1:T(8,128)} async-done(((f32[2,2,256,256]{3,2,0,1:T(8,128)}), f32[32,2,256,256]{3,2,0,1:T(8,128)}) %all-gather.12.cloned.1.call-update) | async-done | bytes 16777232 | tf_op jit(solution)/shard_map/all_gather | solution.py:160
  414.3 7.0 reduce_sum.113
  424.8 2.4 maximum_maximum_fusion.1
  427.3 12.6 %while.37 = (s32[]{:T(128)}, bf16[2,640,640]{2,1,0:T(8,128)(2,1)}, s32[4,3]{1,0:T(4,128)S(1)}, bf16[4,2,256,256]{3,2,1,0:T(8,128)(2,1)S(1)}, s32[]{:T(128)}) while((s32[]{:T(128)}, bf16[2,640,640]{2,1,0:T(8,128)(2,1)}, s32[4,3]{1,0:T(4,128)S(1)}, bf16[4,2,256,256]{3,2,1,0:T(8,128)(2,1)S(1)}, s32[]{:T(128)}) %tuple.166), condition=%wide.while_cond.7, body=%wide.while_body.7.sunk | while | flops 2 | bytes 524405 | solution.py:109
  428.1 2.5 bitcast_dynamic-update-slice_fusion.5
  431.3 2.5 bitcast_dynamic-update-slice_fusion.5
  434.4 2.5 bitcast_dynamic-update-slice_fusion.5
  437.4 2.5 bitcast_dynamic-update-slice_fusion.5
  447.0 5.7 subtract_convert_fusion
  452.7 4.8 pad_maximum_fusion.1
  457.5 2.6 convert_element_type.155
  460.1 4.2 convert_bitcast_fusion.1
  464.4 2.8 copy.70
  472.8 4.9 copy.63
  477.7 2.6 convert_element_type.159
  480.3 4.2 convert_bitcast_fusion
  484.5 3.1 copy.71
  494.8 24.8 %while.35 = (s32[]{:T(128)}, f32[2,640,640]{2,1,0:T(8,128)}, s32[2,2]{1,0:T(2,128)S(1)}, f32[2,2,256,256]{3,2,1,0:T(8,128)S(1)}, s32[]{:T(128)}, /*index=5*/s32[]{:T(128)}, s32[]{:T(128)}) while((s32[]{:T(128)}, f32[2,640,640]{2,1,0:T(8,128)}, s32[2,2]{1,0:T(2,128)S(1)}, f32[2,2,256,256]{3,2,1,0:T(8,128)S(1)}, s32[]{:T(128)}, ...), condition=%wide.region_14.15_spmd, body=%wide.region_13.14_spmd.sunk | while | flops 131080 | bytes 2621637 | solution.py:146
  500.6 6.4 dynamic_update_slice.17
  512.8 6.8 dynamic_update_slice.17
  525.5 20.9 %collective-permute-done.9 = bf16[2,256,384]{2,1,0:T(8,128)(2,1)S(1)} collective-permute-done((bf16[2,256,384]{2,1,0:T(8,128)(2,1)S(1)}, bf16[2,256,384]{2,1,0:T(8,128)(2,1)S(1)}, u32[]{:S(2)}, u32[]{:S(2)}) %collective-permute-start.9) | collective-permute-done | bytes 393248 | tf_op jit(solution)/shard_map/ppermute | solution.py:16
  546.8 6.8 collective-permute-start.11
  554.7 11.6 %collective-permute-done.11 = bf16[2,384,256]{2,1,0:T(8,128)(2,1)S(1)} collective-permute-done((bf16[2,384,256]{2,1,0:T(8,128)(2,1)S(1)}, bf16[2,384,256]{2,1,0:T(8,128)(2,1)S(1)}, u32[]{:S(2)}, u32[]{:S(2)}) %collective-permute-start.11) | collective-permute-done | bytes 393248 | tf_op jit(solution)/shard_map/ppermute | solution.py:16
  567.3 18.6 %all-reduce.7.cloned.1.call-done = (bf16[2,384,384]{2,1,0:T(8,128)(2,1)}, bf16[4,2,256,256]{3,2,0,1:T(8,128)(2,1)}) async-done(((bf16[2,384,384]{2,1,0:T(8,128)(2,1)}, bf16[4,2,256,256]{3,2,0,1:T(8,128)(2,1)}), (bf16[2,384,384]{2,1,0:T(8,128)(2,1)}, bf16[4,2,256,256]{3,2,0,1:T(8,128)(2,1)})) %all-reduce.7.cloned.1.call-update) | async-done | bytes 1638416 | tf_op jit(solution)/shard_map/psum | solution.py:159
  589.3 192.0 %all-gather.14.cloned.1.call-done = f32[32,2,256,256]{3,2,0,1:T(8,128)} async-done(((f32[2,2,256,256]{3,2,0,1:T(8,128)}), f32[32,2,256,256]{3,2,0,1:T(8,128)}) %all-gather.14.cloned.1.call-update) | async-done | bytes 16777232 | tf_op jit(solution)/shard_map/all_gather | solution.py:160
  781.4 7.1 reduce_sum.119
  (221 shorter events, 93.0 us)
Async XLA Ops:
  7.2 49.8 %all-gather.8.cloned.1.call-start = ((), (), s32[]{:S(2)}) async-start(), calls=%async_computation | async-start | bytes 3145728 | tf_op jit(solution)/shard_map/all_gather | solution.py:120
  8.5 11.2 %copy-start.31 = (s32[4,2]{0,1:T(2,128)S(1)}, s32[4,2]{0,1:T(2,128)}, u32[]{:S(2)}) copy-start(s32[4,2]{0,1:T(2,128)} %param.27) | copy-start | bytes 100
  8.6 11.4 %copy-start.33 = (s32[4]{0:T(128)S(1)}, s32[4]{0:T(128)}, u32[]{:S(2)}) copy-start(s32[4]{0:T(128)} %param.29) | copy-start | bytes 52
  8.6 11.6 %copy-start.32 = (f32[8,2]{0,1:T(2,128)S(1)}, f32[8,2]{0,1:T(2,128)}, u32[]{:S(2)}) copy-start(f32[8,2]{0,1:T(2,128)} %param.25) | copy-start | bytes 196
  8.6 34.2 %collective-permute-start = (bf16[2,384,256]{2,1,0:T(8,128)(2,1)S(1)}, bf16[2,384,256]{2,1,0:T(8,128)(2,1)S(1)}, u32[]{:S(2)}, u32[]{:S(2)}) collective-permute-start(bf16[2,384,256]{2,1,0:T(8,128)(2,1)S(1)} %slice.449), channel_id=1, source_target_pairs={{0,30},{2,0},{4,2},{6,4},{8,6},{10,8},{12,10},{14,12},{16,14},{18,... | collective-permute-start | bytes 1179656 | tf_op jit(solution)/shard_map/ppermute | solution.py:16
  15.7 30.7 %collective-permute-start.1 = (bf16[2,256,384]{2,1,0:T(8,128)(2,1)S(1)}, bf16[2,256,384]{2,1,0:T(8,128)(2,1)S(1)}, u32[]{:S(2)}, u32[]{:S(2)}) collective-permute-start(bf16[2,256,384]{2,1,0:T(8,128)(2,1)S(1)} %slice.450), channel_id=1, source_target_pairs={{0,16},{2,18},{4,20},{6,22},{8,24},{10,26},{12,28},{14,30},{16,0},... | collective-permute-start | bytes 1179656 | tf_op jit(solution)/shard_map/ppermute | solution.py:16
  15.8 27.0 %collective-permute-start.2 = (bf16[2,256,256]{2,1,0:T(8,128)(2,1)S(1)}, bf16[2,256,256]{2,1,0:T(8,128)(2,1)S(1)}, u32[]{:S(2)}, u32[]{:S(2)}) collective-permute-start(bf16[2,256,256]{2,1,0:T(8,128)(2,1)S(1)} %slice.451), channel_id=1, source_target_pairs={{0,14},{2,16},{4,18},{6,20},{8,22},{10,24},{12,26},{14,28},{16,30}... | collective-permute-start | bytes 786440 | tf_op jit(solution)/shard_map/ppermute | solution.py:16
  16.9 179.5 %all-reduce.9.cloned.1.call-start = ((), (), s32[]{:S(2)}) async-start(), calls=%async_computation.5 | async-start | bytes 3276800 | tf_op jit(solution)/shard_map/psum | solution.py:159
  54.8 2.2 copy-start.15
  54.8 2.2 copy-start.17
  58.7 1.7 copy-start.9
  70.7 2.6 copy-start.30
  82.6 1.2 copy-start.27
  90.9 2.6 copy-start.25
  102.4 1.3 copy-start.16
  102.4 1.5 copy-start.18
  132.8 28.4 %copy-start = (f32[2,640,640]{2,1,0:T(8,128)S(1)}, f32[2,640,640]{2,1,0:T(8,128)}, u32[]{:S(2)}) copy-start(f32[2,640,640]{2,1,0:T(8,128)} %get-tuple-element.232) | copy-start | bytes 9830404
  135.1 26.1 %collective-permute-start.3 = (bf16[2,256,384]{2,1,0:T(8,128)(2,1)S(1)}, bf16[2,256,384]{2,1,0:T(8,128)(2,1)S(1)}, u32[]{:S(2)}, u32[]{:S(2)}) collective-permute-start(bf16[2,256,384]{2,1,0:T(8,128)(2,1)S(1)} %slice.463), channel_id=1, source_target_pairs={{0,16},{2,18},{4,20},{6,22},{8,24},{10,26},{12,28},{14,30},{16,0},... | collective-permute-start | bytes 1179656 | tf_op jit(solution)/shard_map/ppermute | solution.py:16
  135.2 32.3 %copy-start.24 = (bf16[4,256,256]{2,1,0:T(8,128)(2,1)S(1)}, bf16[4,256,256]{2,1,0:T(8,128)(2,1)}, u32[]{:S(2)}) copy-start(bf16[4,256,256]{2,1,0:T(8,128)(2,1)} %get-tuple-element.259) | copy-start | bytes 1572868
  135.2 26.2 %collective-permute-start.4 = (bf16[2,256,256]{2,1,0:T(8,128)(2,1)S(1)}, bf16[2,256,256]{2,1,0:T(8,128)(2,1)S(1)}, u32[]{:S(2)}, u32[]{:S(2)}) collective-permute-start(bf16[2,256,256]{2,1,0:T(8,128)(2,1)S(1)} %slice.465), channel_id=1, source_target_pairs={{0,18},{2,20},{4,22},{6,24},{8,26},{10,28},{12,30},{14,0},{16,2},{... | collective-permute-start | bytes 786440 | tf_op jit(solution)/shard_map/ppermute | solution.py:16
  161.6 13.6 %collective-permute-start.5 = (bf16[2,384,256]{2,1,0:T(8,128)(2,1)S(1)}, bf16[2,384,256]{2,1,0:T(8,128)(2,1)S(1)}, u32[]{:S(2)}, u32[]{:S(2)}) collective-permute-start(bf16[2,384,256]{2,1,0:T(8,128)(2,1)S(1)} %slice.531), channel_id=1, source_target_pairs={{0,2},{2,4},{4,6},{6,8},{8,10},{10,12},{12,14},{14,16},{16,18},{18... | collective-permute-start | bytes 1179656 | tf_op jit(solution)/shard_map/ppermute | solution.py:16
  168.6 7.6 copy-start.34
  175.3 23.3 %copy-start.2 = (f32[1,2,384,384]{3,2,1,0:T(8,128)S(1)}, f32[1,2,384,384]{3,2,1,0:T(8,128)}, u32[]{:S(2)}) copy-start(f32[1,2,384,384]{3,2,1,0:T(8,128)} %param.23) | copy-start | bytes 3538948
  176.1 238.2 %all-gather.12.cloned.1.call-start = ((), (), s32[]{:S(2)}) async-start(), calls=%async_computation.2 | async-start | bytes 17825792 | tf_op jit(solution)/shard_map/all_gather | solution.py:160
  196.4 2.2 copy-start.21
  198.6 243.7 %all-gather.10.cloned.1.call-start = ((), (), s32[]{:S(2)}) async-start(), calls=%async_computation.1 | async-start | bytes 3145728 | tf_op jit(solution)/shard_map/all_gather | solution.py:120
  201.1 223.6 %collective-permute-start.6 = (bf16[2,384,256]{2,1,0:T(8,128)(2,1)}, bf16[2,384,256]{2,1,0:T(8,128)(2,1)S(1)}, u32[]{:S(2)}, u32[]{:S(2)}) collective-permute-start(bf16[2,384,256]{2,1,0:T(8,128)(2,1)} %slice.470), channel_id=1, source_target_pairs={{0,30},{2,0},{4,2},{6,4},{8,6},{10,8},{12,10},{14,12},{16,14},{18,... | collective-permute-start | bytes 1179656 | tf_op jit(solution)/shard_map/ppermute | solution.py:16
  206.6 218.2 %collective-permute-start.7 = (bf16[2,256,384]{2,1,0:T(8,128)(2,1)}, bf16[2,256,384]{2,1,0:T(8,128)(2,1)}, u32[]{:S(2)}, u32[]{:S(2)}) collective-permute-start(bf16[2,256,384]{2,1,0:T(8,128)(2,1)} %slice.471), channel_id=1, source_target_pairs={{0,16},{2,18},{4,20},{6,22},{8,24},{10,26},{12,28},{14,30},{16,0},... | collective-permute-start | bytes 1179656 | tf_op jit(solution)/shard_map/ppermute | solution.py:16
  206.6 218.2 %collective-permute-start.8 = (bf16[2,256,256]{2,1,0:T(8,128)(2,1)}, bf16[2,256,256]{2,1,0:T(8,128)(2,1)}, u32[]{:S(2)}, u32[]{:S(2)}) collective-permute-start(bf16[2,256,256]{2,1,0:T(8,128)(2,1)} %slice.472), channel_id=1, source_target_pairs={{0,14},{2,16},{4,18},{6,20},{8,22},{10,24},{12,26},{14,28},{16,30}... | collective-permute-start | bytes 786440 | tf_op jit(solution)/shard_map/ppermute | solution.py:16
  424.7 161.1 %all-reduce.7.cloned.1.call-start = ((), (), s32[]{:S(2)}) async-start(), calls=%async_computation.4 | async-start | bytes 3276800 | tf_op jit(solution)/shard_map/psum | solution.py:159
  440.1 2.2 copy-start.11
  440.1 2.2 copy-start.13
  444.1 2.9 copy-start.5
  444.1 2.9 copy-start.7
  469.3 1.2 copy-start.28
  477.7 2.6 copy-start.26
  488.9 1.5 copy-start.8
  488.9 1.7 copy-start.12
  488.9 1.8 copy-start.14
  519.6 26.8 %copy-start.1 = (f32[2,640,640]{2,1,0:T(8,128)S(1)}, f32[2,640,640]{2,1,0:T(8,128)}, u32[]{:S(2)}) copy-start(f32[2,640,640]{2,1,0:T(8,128)} %get-tuple-element.233) | copy-start | bytes 9830404
  521.9 24.5 %collective-permute-start.9 = (bf16[2,256,384]{2,1,0:T(8,128)(2,1)S(1)}, bf16[2,256,384]{2,1,0:T(8,128)(2,1)S(1)}, u32[]{:S(2)}, u32[]{:S(2)}) collective-permute-start(bf16[2,256,384]{2,1,0:T(8,128)(2,1)S(1)} %slice.484), channel_id=1, source_target_pairs={{0,16},{2,18},{4,20},{6,22},{8,24},{10,26},{12,28},{14,30},{16,0},... | collective-permute-start | bytes 1179656 | tf_op jit(solution)/shard_map/ppermute | solution.py:16
  523.4 30.2 %copy-start.23 = (bf16[4,256,256]{2,1,0:T(8,128)(2,1)S(1)}, bf16[4,256,256]{2,1,0:T(8,128)(2,1)}, u32[]{:S(2)}) copy-start(bf16[4,256,256]{2,1,0:T(8,128)(2,1)} %get-tuple-element.257) | copy-start | bytes 1572868
  523.4 23.3 %collective-permute-start.10 = (bf16[2,256,256]{2,1,0:T(8,128)(2,1)S(1)}, bf16[2,256,256]{2,1,0:T(8,128)(2,1)S(1)}, u32[]{:S(2)}, u32[]{:S(2)}) collective-permute-start(bf16[2,256,256]{2,1,0:T(8,128)(2,1)S(1)} %slice.486), channel_id=1, source_target_pairs={{0,18},{2,20},{4,22},{6,24},{8,26},{10,28},{12,30},{14,0},{16,2},{... | collective-permute-start | bytes 786440 | tf_op jit(solution)/shard_map/ppermute | solution.py:16
  546.8 19.5 %collective-permute-start.11 = (bf16[2,384,256]{2,1,0:T(8,128)(2,1)S(1)}, bf16[2,384,256]{2,1,0:T(8,128)(2,1)S(1)}, u32[]{:S(2)}, u32[]{:S(2)}) collective-permute-start(bf16[2,384,256]{2,1,0:T(8,128)(2,1)S(1)} %slice.530), channel_id=1, source_target_pairs={{0,2},{2,4},{4,6},{6,8},{8,10},{10,12},{12,14},{14,16},{16,18},{18... | collective-permute-start | bytes 1179656 | tf_op jit(solution)/shard_map/ppermute | solution.py:16
  566.4 21.6 %copy-start.22 = (bf16[2,384,384]{2,1,0:T(8,128)(2,1)S(1)}, bf16[2,384,384]{2,1,0:T(8,128)(2,1)}, u32[]{:S(2)}) copy-start(bf16[2,384,384]{2,1,0:T(8,128)(2,1)} %get-tuple-element.298) | copy-start | bytes 1769476
  567.3 214.1 %all-gather.14.cloned.1.call-start = ((), (), s32[]{:S(2)}) async-start(), calls=%async_computation.3 | async-start | bytes 17825792 | tf_op jit(solution)/shard_map/all_gather | solution.py:160
  585.9 2.2 copy-start.29
  781.4 7.1 copy-start.4
  (5 other events, 5.1 us)
Sparse Core Ops, SparseCore 0:
  17.1 9.6 all-gather.7
  176.3 20.1 all-reduce.8
  199.8 214.5 all-gather.11
  424.9 8.7 all-gather.9
  567.4 18.4 all-reduce.6
  589.1 192.2 all-gather.13
